TPU v7x, 32 devices: a whole 2x2x4 slice. The times are simulated.
32 devices in a mesh: dp: 16 (over z, y, x), tensor: 2 (over core).
Axes of the slice: x: 2, y: 2, z: 4, core: 2. Of those that a mesh axis runs over, the one named last changes fastest.
Arguments:
- tokens_in: bfloat16 [32768, 768], P('dp'), may hold values from -6 to 6
- segment_ids: int32 [64, 512], P('dp'), may hold values from 0 to 3, never falling along the last dimension, each value on 1 to 256 neighbouring positions
- w_qkv: bfloat16 [3, 768, 768], P(None, None, 'tensor'), may hold values from -0.3125 to 0.3125
- bias_qv: bfloat16 [2, 768], P(None, 'tensor'), may hold values from -1.796875 to 1.796875
- w_out: bfloat16 [768, 768], P('tensor'), may hold values from -0.875 to 0.875
- bias_out: bfloat16 [768], replicated, may hold values from -1.796875 to 1.796875
- norm1_gain: bfloat16 [768], replicated, may hold values from 0.25 to 1.75
- norm1_shift: bfloat16 [768], replicated, may hold values from -1.796875 to 1.796875
- w_in: bfloat16 [768, 3072], P(None, 'tensor'), may hold values from -0.21875 to 0.21875
- bias_in: bfloat16 [3072], P('tensor'), may hold values from -1.796875 to 1.796875
- w_down: bfloat16 [3072, 768], P('tensor'), may hold values from -0.15625 to 0.15625
- bias_down: bfloat16 [768], replicated, may hold values from -1.796875 to 1.796875
- norm2_gain: bfloat16 [768], replicated, may hold values from 0.25 to 1.75
- norm2_shift: bfloat16 [768], replicated, may hold values from -1.796875 to 1.796875
- grad_output: bfloat16 [32768, 768], P('dp'), may hold values from -6 to 6
Outputs:
- output: bfloat16 [32768, 768], P('dp')
- grad_input: bfloat16 [32768, 768], P('dp')
- grad_w_qkv: float32 [3, 768, 768], P(None, 'dp', 'tensor')
- grad_bias_qv: float32 [2, 768], P(None, 'tensor')
- grad_w_out: float32 [768, 768], P('tensor', 'dp')
- grad_bias_out: float32 [768], replicated
- grad_norm1_gain: float32 [768], replicated
- grad_norm1_shift: float32 [768], replicated
- grad_w_in: float32 [768, 3072], P('dp', 'tensor')
- grad_bias_in: float32 [3072], P('tensor')
- grad_w_down: float32 [3072, 768], P('tensor', 'dp')
- grad_bias_down: float32 [768], replicated
- grad_norm2_gain: float32 [768], replicated
- grad_norm2_shift: float32 [768], replicated
Inputs may be any that keep to these rules, and one draw needn't show every extreme that they name: `segment_ids`: within each sequence the page numbers never fall; every page 0 to 3 is present, with 1 to 256 tokens.
All inputs are finite; a program needn't handle non-finite values.
Results may differ from a plain program's by a relative error of at most 0.02.
The roundings to bfloat16 on the way count: a program that leaves them out, or rounds other values in their place, can miss the bound.
Values may be sent and summed in bfloat16 or wider, within the bound.
No kernel may reach another device: no remote copies, remote signals or barrier semaphores. Data moves between devices by JAX's collectives and lax.ppermute only.
A program may use at most 192 MiB of HBM per device.

v0:
```python
import math
import jax
import jax.numpy as jnp
from jax import lax
from jax.sharding import PartitionSpec as P

HEAD_DIM = 64
EPSILON = 1e-05
NEGATIVE = -1e30
ROOT_HALF = 0.7071067811865476
ROOT_TWO_PI_INV = 0.3989422804014327


def norm_forward(summed, gain_vec, shift_vec):
    centered = summed - jnp.mean(summed, axis=-1, keepdims=True)
    variance = jnp.mean(centered * centered, axis=-1, keepdims=True)
    inv_std = lax.rsqrt(variance + EPSILON)
    normed = centered * inv_std
    return (normed * gain_vec + shift_vec, normed, inv_std)


def norm_backward(upstream, normed, inv_std, gain_vec):
    scaled_grad = upstream * gain_vec
    first_mean = jnp.mean(scaled_grad, axis=-1, keepdims=True)
    second_mean = jnp.mean(scaled_grad * normed, axis=-1, keepdims=True)
    grad_summed = inv_std * (scaled_grad - first_mean - normed * second_mean)
    return (grad_summed, jnp.sum(upstream * normed, axis=0), jnp.sum(upstream, axis=0))


def gelu_pair(preact):
    cumulative = 0.5 * (1.0 + lax.erf(preact * ROOT_HALF))
    derivative = cumulative + preact * jnp.exp(-0.5 * preact * preact) * ROOT_TWO_PI_INV
    return (preact * cumulative, derivative)


def shards(
    tokens_in,
    segment_ids,
    w_qkv,
    bias_qv,
    w_out,
    bias_out,
    norm1_gain,
    norm1_shift,
    w_in,
    bias_in,
    w_down,
    bias_down,
    norm2_gain,
    norm2_shift,
    grad_output,
):
    seq_count, seq_length = segment_ids.shape
    local_cols = w_qkv.shape[2]
    head_count = local_cols // HEAD_DIM
    row_count = tokens_in.shape[0]
    scaling = 1.0 / math.sqrt(HEAD_DIM)
    shape_four = (seq_count, seq_length, head_count, HEAD_DIM)
    same_page = segment_ids[:, :, None] == segment_ids[:, None, :]

    def masked_scores(seq_query, seq_keys, page_mask):
        scores = (
            jnp.einsum("qhd,khd->hqk", seq_query, seq_keys, preferred_element_type=jnp.float32)
            * scaling
        )
        return jnp.where(page_mask[None], scores, NEGATIVE)

    def attend_forward(operands):
        seq_query, seq_keys, seq_values, page_mask = operands
        scores = masked_scores(seq_query, seq_keys, page_mask)
        row_max = jnp.max(scores, axis=-1, keepdims=True)
        exp_scores = jnp.exp(scores - row_max)
        row_sum = jnp.sum(exp_scores, axis=-1, keepdims=True)
        weights_low = (exp_scores / row_sum).astype(jnp.bfloat16)
        context = jnp.einsum(
            "hqk,khd->qhd", weights_low, seq_values, preferred_element_type=jnp.float32
        )
        return (context.astype(jnp.bfloat16), (row_max + jnp.log(row_sum))[..., 0])

    def attend_backward(operands):
        seq_query, seq_keys, seq_values, page_mask, log_norm, grad_context = operands
        scores = masked_scores(seq_query, seq_keys, page_mask)
        probs = jnp.exp(scores - log_norm[..., None])
        grad_values = jnp.einsum(
            "hqk,qhd->khd",
            probs.astype(jnp.bfloat16),
            grad_context,
            preferred_element_type=jnp.float32,
        )
        grad_probs = jnp.einsum(
            "qhd,khd->hqk", grad_context, seq_values, preferred_element_type=jnp.float32
        )
        row_dot = jnp.sum(probs * grad_probs, axis=-1, keepdims=True)
        grad_scores = (probs * (grad_probs - row_dot)).astype(jnp.bfloat16)
        grad_query = (
            jnp.einsum("hqk,khd->qhd", grad_scores, seq_keys, preferred_element_type=jnp.float32)
            * scaling
        )
        grad_keys = (
            jnp.einsum("hqk,qhd->khd", grad_scores, seq_query, preferred_element_type=jnp.float32)
            * scaling
        )
        return (
            grad_query.astype(jnp.bfloat16),
            grad_keys.astype(jnp.bfloat16),
            grad_values.astype(jnp.bfloat16),
        )

    tokens_f32 = tokens_in.astype(jnp.float32)
    projected = jnp.einsum("nd,jdc->jnc", tokens_in, w_qkv, preferred_element_type=jnp.float32)
    query_low = (projected[0] + bias_qv[0]).astype(jnp.bfloat16).reshape(shape_four)
    keys_low = projected[1].astype(jnp.bfloat16).reshape(shape_four)
    values_low = (projected[2] + bias_qv[1]).astype(jnp.bfloat16).reshape(shape_four)
    context, log_norm = lax.map(attend_forward, (query_low, keys_low, values_low, same_page))
    context_flat = context.reshape(row_count, local_cols)
    attention_part = jnp.dot(context_flat, w_out, preferred_element_type=jnp.float32)
    attention = lax.psum(attention_part.astype(jnp.bfloat16), "tensor").astype(jnp.float32)
    normed_one, normed1, inv_std_one = norm_forward(
        tokens_f32 + attention + bias_out, norm1_gain, norm1_shift
    )
    normed_low = normed_one.astype(jnp.bfloat16)
    preact = jnp.dot(normed_low, w_in, preferred_element_type=jnp.float32) + bias_in
    hidden, derivative = gelu_pair(preact)
    hidden_low = hidden.astype(jnp.bfloat16)
    feedforward_part = jnp.dot(hidden_low, w_down, preferred_element_type=jnp.float32)
    feedforward = lax.psum(feedforward_part.astype(jnp.bfloat16), "tensor").astype(jnp.float32)
    result, normed2, inv_std_two = norm_forward(
        normed_one + feedforward + bias_down, norm2_gain, norm2_shift
    )
    output = result.astype(jnp.bfloat16)
    upstream = grad_output.astype(jnp.float32)
    grad_summed_two, grad_gain_two, grad_shift_two = norm_backward(
        upstream, normed2, inv_std_two, norm2_gain
    )
    grad_bias_down = jnp.sum(grad_summed_two, axis=0)
    grad_two_low = grad_summed_two.astype(jnp.bfloat16)
    grad_w_down = jnp.einsum(
        "nf,nd->fd", hidden_low, grad_two_low, preferred_element_type=jnp.float32
    )
    grad_hidden = jnp.einsum("nd,fd->nf", grad_two_low, w_down, preferred_element_type=jnp.float32)
    grad_preact = (grad_hidden * derivative).astype(jnp.bfloat16)
    grad_bias_in = jnp.sum(grad_preact, axis=0, dtype=jnp.float32)
    grad_w_in = jnp.einsum("nd,nf->df", normed_low, grad_preact, preferred_element_type=jnp.float32)
    normed_part = jnp.einsum("nf,df->nd", grad_preact, w_in, preferred_element_type=jnp.float32)
    grad_normed_one = grad_summed_two + lax.psum(normed_part.astype(jnp.bfloat16), "tensor").astype(
        jnp.float32
    )
    grad_summed_one, grad_gain_one, grad_shift_one = norm_backward(
        grad_normed_one, normed1, inv_std_one, norm1_gain
    )
    grad_bias_out = jnp.sum(grad_summed_one, axis=0)
    grad_one_low = grad_summed_one.astype(jnp.bfloat16)
    grad_w_out = jnp.einsum(
        "nc,nd->cd", context_flat, grad_one_low, preferred_element_type=jnp.float32
    )
    grad_context = jnp.einsum(
        "nd,cd->nc", grad_one_low, w_out, preferred_element_type=jnp.float32
    ).astype(jnp.bfloat16)
    grad_query, grad_keys, grad_values = lax.map(
        attend_backward,
        (query_low, keys_low, values_low, same_page, log_norm, grad_context.reshape(shape_four)),
    )
    grad_stack = jnp.stack(
        [
            grad_query.reshape(row_count, local_cols),
            grad_keys.reshape(row_count, local_cols),
            grad_values.reshape(row_count, local_cols),
        ]
    )
    grad_w_qkv = jnp.einsum(
        "nd,jnc->jdc", tokens_in, grad_stack, preferred_element_type=jnp.float32
    )
    grad_bias_qv = jnp.stack(
        [
            jnp.sum(grad_stack[0], axis=0, dtype=jnp.float32),
            jnp.sum(grad_stack[2], axis=0, dtype=jnp.float32),
        ]
    )
    input_part = jnp.einsum("jnc,jdc->nd", grad_stack, w_qkv, preferred_element_type=jnp.float32)
    grad_input = (
        grad_summed_one + lax.psum(input_part.astype(jnp.bfloat16), "tensor").astype(jnp.float32)
    ).astype(jnp.bfloat16)
    summed_w_qkv, summed_w_out, summed_w_in, summed_w_down = (
        lax.psum_scatter(grad_w_qkv, "dp", scatter_dimension=1, tiled=True),
        lax.psum_scatter(grad_w_out, "dp", scatter_dimension=1, tiled=True),
        lax.psum_scatter(grad_w_in, "dp", scatter_dimension=0, tiled=True),
        lax.psum_scatter(grad_w_down, "dp", scatter_dimension=1, tiled=True),
    )
    (
        summed_bias_qv,
        summed_bias_out,
        summed_gain_one,
        summed_shift_one,
        summed_bias_in,
        summed_bias_down,
        summed_gain_two,
        summed_shift_two,
    ) = lax.psum(
        (
            grad_bias_qv,
            grad_bias_out,
            grad_gain_one,
            grad_shift_one,
            grad_bias_in,
            grad_bias_down,
            grad_gain_two,
            grad_shift_two,
        ),
        "dp",
    )
    return (
        output,
        grad_input,
        summed_w_qkv,
        summed_bias_qv,
        summed_w_out,
        summed_bias_out,
        summed_gain_one,
        summed_shift_one,
        summed_w_in,
        summed_bias_in,
        summed_w_down,
        summed_bias_down,
        summed_gain_two,
        summed_shift_two,
    )


def solution(mesh):
    return jax.shard_map(
        shards,
        mesh=mesh,
        in_specs=(
            P("dp", None),
            P("dp", None),
            P(None, None, "tensor"),
            P(None, "tensor"),
            P("tensor", None),
            P(),
            P(),
            P(),
            P(None, "tensor"),
            P("tensor"),
            P("tensor", None),
            P(),
            P(),
            P(),
            P("dp", None),
        ),
        out_specs=(
            P("dp", None),
            P("dp", None),
            P(None, "dp", "tensor"),
            P(None, "tensor"),
            P("tensor", "dp"),
            P(),
            P(),
            P(),
            P("dp", "tensor"),
            P("tensor"),
            P("tensor", "dp"),
            P(),
            P(),
            P(),
        ),
        check_vma=False,
    )
```

profile of v0, /device:TPU:0, one launch (start us, length us, event | category | flops | bytes accessed | tf_op | source)
XLA Modules:
  0.0 976.2 jit_solution(554797864243387080)
XLA Ops:
  7.2 6.5 convolution_bitcast_fusion
  18.2 5.4 squeeze.37
  23.6 5.2 squeeze.38
  29.1 3.8 convert_element_type.141
  36.6 6.5 fusion.77
  44.4 29.8 %while.26 = (s32[]{:T(128)}, bf16[4,512,6,64]{1,3,2,0:T(8,128)(2,1)}, f32[4,6,512]{2,1,0:T(8,128)S(1)}, bf16[4,512,6,64]{1,3,2,0:T(8,128)(2,1)}, pred[4,512,512]...) while((s32[]{:T(128)}, ...), condition=%wide.region_3.4_spmd, body=%wide.region_0.3_spmd.sunk | while | flops 421721088 | bytes 21870684 | solution.py:114
  82.4 25.9 %all-reduce.8.cloned.1.call-done = bf16[2048,768]{1,0:T(8,128)(2,1)} async-done(((bf16[2048,768]{1,0:T(8,128)(2,1)}), bf16[2048,768]{1,0:T(8,128)(2,1)}) %all-reduce.8.cloned.1.call-update) | async-done | bytes 3145744 | tf_op jit(solution)/shard_map/psum | solution.py:117
  108.3 4.1 fusion.73
  114.8 9.6 multiply_convert_fusion.1
  127.1 6.4 convolution_convert_fusion.2
  133.6 24.4 %all-reduce.10.cloned.1.call-done = bf16[2048,768]{1,0:T(8,128)(2,1)} async-done(((bf16[2048,768]{1,0:T(8,128)(2,1)}), bf16[2048,768]{1,0:T(8,128)(2,1)}) %all-reduce.10.cloned.1.call-update) | async-done | bytes 3145744 | tf_op jit(solution)/shard_map/psum | solution.py:126
  158.0 5.6 fusion.96
  173.0 13.6 %convert_reduce_fusion = (f32[1536]{0:T(1024)}, bf16[2048,1536]{1,0:T(8,128)(2,1)S(1)}) fusion(f32[2048,1536]{1,0:T(8,128)} %get-tuple-element.270, f32[1536]{0:T(1024)S(1)} %convert_element_type.148, bf16[1536,768]{1,0:T(8,128)(2,1)S(1)} %copy-done.32, f32[2048,768]{1,0:T(8,128)S(1)} %get-tuple-element.267), kind=kOutput, calls=%fused_computation.71 | convolution fusion | flops 4874304000 | bytes 27537408 | tf_op jit(solution)/shard_map/nd,fd->nf/dot_general | solution.py:140
  189.3 6.4 convolution_convert_fusion.1
  195.8 24.5 %all-reduce.12.cloned.1.call-done = bf16[2048,768]{1,0:T(8,128)(2,1)} async-done(((bf16[2048,768]{1,0:T(8,128)(2,1)}), bf16[2048,768]{1,0:T(8,128)(2,1)}) %all-reduce.12.cloned.1.call-update) | async-done | bytes 3145744 | tf_op jit(solution)/shard_map/psum | solution.py:145
  220.3 8.9 multiply_reduce_fusion.1
  229.3 8.2 fusion.95
  237.5 4.6 convolution_convert_fusion.3
  252.2 64.4 %while.27 = (s32[]{:T(128)}, bf16[4,512,6,64]{1,3,2,0:T(8,128)(2,1)}, bf16[4,512,6,64]{1,3,2,0:T(8,128)(2,1)}, bf16[4,512,6,64]{1,3,2,0:T(8,128)(2,1)}, bf16[4,5...) while((s32[]{:T(128)}, ...), condition=%wide.region_17.18_spmd, body=%wide.region_15.17_spmd.sunk | while | flops 1031205888 | bytes 52520052 | solution.py:159
  316.6 3.9 copy.76
  334.7 9.1 bitcast_convert_fusion
  343.9 8.5 fusion.79
  352.4 6.3 copy.83
  358.8 6.1 fusion.82
  365.2 12.1 %fusion.88 = f32[768,1536]{1,0:T(8,128)} fusion(bf16[2048,1536]{1,0:T(8,128)(2,1)} %copy-done.35, f32[768]{0:T(1024)S(1)} %copy-done.21, f32[768]{0:T(1024)S(1)} %convert_element_type.145, bf16[2048,768]{1,0:T(8,128)(2,1)} %all-reduce.8.cloned.1.call-done, bf16[2048,768]{1,0:T(8,128)(2,1)S(1)} %copy-done.4, f32[2048]{0:T(1024)S(1)} %add_rsqrt_fusion.1, ...), kind=kOutput, calls=%fused_computation.125 | convolution fusion | flops 4845993984 | bytes 17327104 | tf_op jit(solution)/shard_map/nd,nf->df/dot_general | solution.py:143
  377.4 11.3 %fusion.85 = f32[1536,768]{0,1:T(8,128)} fusion(bf16[2048,1536]{1,0:T(8,128)(2,1)} %copy-done.34, f32[2048,768]{1,0:T(8,128)} %copy-done.7), kind=kOutput, calls=%fused_computation.122 | convolution fusion | flops 4833411072 | bytes 17301504 | tf_op jit(solution)/shard_map/nf,nd->fd/dot_general | solution.py:137
  392.2 79.8 %all-reduce.1 = (f32[2,384]{1,0:T(2,128)}, f32[768]{0:T(1024)}, f32[768]{0:T(1024)}, f32[768]{0:T(1024)}, f32[1536]{0:T(1024)}, /*index=5*/f32[768]{0:T(1024)}, f32[768]{0:T(1024)}, f32[768]{0:T(1024)}) all-reduce(f32[2,384]{1,0:T(2,128)S(1)} %pad_maximum_fusion.3, ...), channel_id=1, replica_groups=mesh['dp'=16,'tensor'=2] {'dp'}, use_global_device_ids=true, to_apply=%region_22.23 | all-reduce | flops 6912 | bytes 55296 | tf_op jit(solution)/shard_map/psum | solution.py:198
  471.9 6.1 add_convert_fusion
  478.0 77.7 %all-reduce.16.cloned.1.call-done = f32[3,768,384]{2,0,1:T(4,128)} async-done(((f32[3,768,384]{2,0,1:T(4,128)}), f32[3,768,384]{2,0,1:T(4,128)}) %all-reduce.16.cloned.1.call-update) | async-done | bytes 3538960
  557.4 126.8 %reduce-scatter.4.cloned.1.call-done = f32[384,48]{0,1:T(8,128)} async-done(((f32[384,768]{0,1:T(8,128)}), f32[384,48]{0,1:T(8,128)}) %reduce-scatter.4.cloned.1.call-update) | async-done | bytes 73744 | tf_op jit(solution)/shard_map/reduce_scatter | solution.py:185
  684.2 142.7 %reduce-scatter.6.cloned.1.call-done = f32[48,1536]{1,0:T(8,128)} async-done(((f32[768,1536]{1,0:T(8,128)}), f32[48,1536]{1,0:T(8,128)}) %reduce-scatter.6.cloned.1.call-update) | async-done | bytes 294928 | tf_op jit(solution)/shard_map/reduce_scatter | solution.py:186
  826.9 142.0 %reduce-scatter.8.cloned.1.call-done = f32[1536,48]{0,1:T(8,128)} async-done(((f32[1536,768]{0,1:T(8,128)}), f32[1536,48]{0,1:T(8,128)}) %reduce-scatter.8.cloned.1.call-update) | async-done | bytes 294928 | tf_op jit(solution)/shard_map/reduce_scatter | solution.py:187
  (194 shorter events, 157.7 us)
Async XLA Ops:
  7.2 107.6 %copy-start = (bf16[768,1536]{1,0:T(8,128)(2,1)S(1)}, bf16[768,1536]{1,0:T(8,128)(2,1)}, u32[]{:S(2)}) copy-start(bf16[768,1536]{1,0:T(8,128)(2,1)} %param.27) | copy-start | bytes 7077892
  7.2 101.1 %all-reduce.8.cloned.1.call-start = ((), (), s32[]{:S(2)}) async-start(), calls=%async_computation.3 | async-start | bytes 6291456 | tf_op jit(solution)/shard_map/psum | solution.py:117
  18.2 10.7 %copy-start.23 = (bf16[2,384]{1,0:T(2,128)(2,1)S(1)}, bf16[2,384]{1,0:T(2,128)(2,1)}, u32[]{:S(2)}) copy-start(bf16[2,384]{1,0:T(2,128)(2,1)} %param.22) | copy-start | bytes 4612
  23.6 12.2 %copy-start.17 = (s32[4,512]{1,0:T(4,128)S(1)}, s32[4,512]{1,0:T(4,128)}, u32[]{:S(2)}) copy-start(s32[4,512]{1,0:T(4,128)} %param.20) | copy-start | bytes 24580
  74.1 8.1 copy-start.10
  77.6 4.7 copy-start.26
  77.6 4.7 copy-start.27
  77.7 4.7 copy-start.24
  82.3 75.7 %all-reduce.10.cloned.1.call-start = ((), (), s32[]{:S(2)}) async-start(), calls=%async_computation.4 | async-start | bytes 6291456 | tf_op jit(solution)/shard_map/psum | solution.py:126
  82.4 75.6 %copy-start.20 = (f32[768]{0:T(1024)}, f32[768]{0:T(1024)S(1)}, u32[]{:S(2)}) copy-start(f32[768]{0:T(1024)S(1)} %convert_element_type.146) | copy-start | bytes 9220
  114.8 12.3 %copy-start.31 = (bf16[1536,768]{1,0:T(8,128)(2,1)S(1)}, bf16[1536,768]{1,0:T(8,128)(2,1)}, u32[]{:S(2)}) copy-start(bf16[1536,768]{1,0:T(8,128)(2,1)} %param.29) | copy-start | bytes 7077892
  127.1 6.5 copy-start.28
  127.1 6.5 copy-start.29
  127.1 6.5 copy-start.30
  133.5 86.8 %all-reduce.12.cloned.1.call-start = ((), (), s32[]{:S(2)}) async-start(), calls=%async_computation.5 | async-start | bytes 6291456 | tf_op jit(solution)/shard_map/psum | solution.py:145
  173.0 13.7 %copy-start.7 = (f32[2048,768]{1,0:T(8,128)}, f32[2048,768]{1,0:T(8,128)S(1)}, u32[]{:S(2)}) copy-start(f32[2048,768]{1,0:T(8,128)S(1)} %get-tuple-element.267) | copy-start | bytes 18874372
  195.7 33.5 %copy-start.3 = (bf16[2048,768]{1,0:T(8,128)(2,1)S(1)}, bf16[2048,768]{1,0:T(8,128)(2,1)}, u32[]{:S(2)}) copy-start(bf16[2048,768]{1,0:T(8,128)(2,1)} %param.19) | copy-start | bytes 9437188
  195.7 276.2 %all-reduce.14.cloned.1.call-start = ((), (), s32[]{:S(2)}) async-start(), calls=%async_computation.6 | async-start | bytes 6291456 | tf_op jit(solution)/shard_map/psum | solution.py:181
  220.3 9.0 copy-start.6
  220.3 9.0 copy-start.12
  229.3 8.2 copy-start.16
  242.8 9.4 copy-start.8
  316.6 8.4 copy-start.13
  334.7 9.2 copy-start.4
  343.8 211.9 %all-reduce.16.cloned.1.call-start = ((), (), s32[]{:S(2)}) async-start(), calls=%async_computation.10 | async-start | bytes 9437184
  358.7 6.5 copy-start.21
  358.7 325.5 %reduce-scatter.4.cloned.1.call-start = ((), (), s32[]{:S(2)}) async-start(), calls=%async_computation.7 | async-start | bytes 1253376 | tf_op jit(solution)/shard_map/reduce_scatter | solution.py:185
  364.9 462.0 %reduce-scatter.6.cloned.1.call-start = ((), (), s32[]{:S(2)}) async-start(), calls=%async_computation.8 | async-start | bytes 5013504 | tf_op jit(solution)/shard_map/reduce_scatter | solution.py:186
  377.3 11.4 %copy-start.33 = (u32[32]{0:T(128)S(1)}, u32[32]{0:T(128)}, u32[]{:S(2)}) copy-start(u32[32]{0:T(128)} %constant.77) | copy-start | bytes 388
  377.3 12.6 %copy-start.9 = (bf16[4,512,6,64]{1,3,2,0:T(8,128)(2,1)S(1)}, bf16[4,512,6,64]{1,3,2,0:T(8,128)(2,1)}, u32[]{:S(2)}) copy-start(bf16[4,512,6,64]{1,3,2,0:T(8,128)(2,1)} %get-tuple-element.108) | copy-start | bytes 4718596
  377.3 591.5 %reduce-scatter.8.cloned.1.call-start = ((), (), s32[]{:S(2)}) async-start(), calls=%async_computation.9 | async-start | bytes 5013504 | tf_op jit(solution)/shard_map/reduce_scatter | solution.py:187
  392.1 576.7 %copy-start.1 = (bf16[768,1536]{1,0:T(8,128)(2,1)S(1)}, bf16[768,1536]{1,0:T(8,128)(2,1)}, u32[]{:S(2)}) copy-start(bf16[768,1536]{1,0:T(8,128)(2,1)} %param.27) | copy-start | bytes 7077892
  (12 other events, 40.6 us)
Sparse Core Ops, SparseCore 0:
  82.4 25.8 all-reduce.7
  133.6 24.3 all-reduce.9
  195.9 24.3 all-reduce.11
  344.0 24.3 all-reduce.13
  374.0 181.7 all-reduce.15
  561.6 122.5 reduce-scatter.3
  690.8 136.0 reduce-scatter.5
  832.6 136.1 reduce-scatter.7
where the time goes:
time: 982 us; the launch traced here: 976 us
  waiting for transfers between devices  564 us (57%)
  matrix products  174 us (18%)
  blocking collectives  79.8 us (8%)
  local copies, waits for them, and re-layouts  75.9 us (8%)
  other arithmetic  65.3 us (7%)
  between operations  15.8 us (2%)
    reduce_scatter x1, waiting for transfers between devices, shards(): lax.psum_scatter(grad_w_in, 'dp', scatter_dimension=0, tiled=True)  143 us
    reduce_scatter x1, waiting for transfers between devices, shards(): lax.psum_scatter(grad_w_down, 'dp', scatter_dimension=1, tiled=True)  142 us
    reduce_scatter x1, waiting for transfers between devices, shards(): lax.psum_scatter(grad_w_out, 'dp', scatter_dimension=1, tiled=True)  127 us
    psum x1, blocking collectives, shards(): lax.psum((grad_bias_qv, grad_bias_out, grad_gain_one, grad_shift_one, gra...  79.8 us
    unnamed x9, waiting for transfers between devices  77.8 us
    psum x1, waiting for transfers between devices, shards(): lax.psum(attention_part.astype(jnp.bfloat16), 'tensor').astype(jnp.float32)  25.9 us
    psum x1, waiting for transfers between devices, shards(): lax.psum(normed_part.astype(jnp.bfloat16), 'tensor').astype(jnp.float32)  24.5 us
    psum x1, waiting for transfers between devices, shards(): lax.psum(feedforward_part.astype(jnp.bfloat16), 'tensor')  24.4 us
  transfers between devices with their start and end apart: 8, of which 7 were waited for; matrix products, arithmetic and copies ran while one was open for 6% of the time, Pallas kernels for 0%

commit v1 on v0

--- a/solution.py
+++ b/solution.py
@@ -123,7 +123,9 @@
     hidden, derivative = gelu_pair(preact)
     hidden_low = hidden.astype(jnp.bfloat16)
     feedforward_part = jnp.dot(hidden_low, w_down, preferred_element_type=jnp.float32)
-    feedforward = lax.psum(feedforward_part.astype(jnp.bfloat16), "tensor").astype(jnp.float32)
+    feedforward = jnp.sum(
+        lax.all_gather(feedforward_part.astype(jnp.bfloat16), "tensor"), axis=0
+    ).astype(jnp.float32)
     result, normed2, inv_std_two = norm_forward(
         normed_one + feedforward + bias_down, norm2_gain, norm2_shift
     )

time: 982 us -> 981 us (level)
    psum x1 -> x0, waiting for transfers between devices: 24.4 us -> none  [shards(): lax.psum(feedforward_part.astype(jnp.bfloat16), 'tensor')]
    all_gather x0 -> x1, waiting for transfers between devices: none -> 18 us  [shards(): lax.all_gather(feedforward_part.astype(jnp.bfloat16), 'tensor')]
where the time goes in v1:
time: 981 us; the launch traced here: 975 us
  waiting for transfers between devices  558 us (57%)
  matrix products  174 us (18%)
  blocking collectives  79.8 us (8%)
  local copies, waits for them, and re-layouts  76.1 us (8%)
  other arithmetic  70.6 us (7%)
  between operations  15.6 us (2%)
    reduce_scatter x1, waiting for transfers between devices, shards(): lax.psum_scatter(grad_w_down, 'dp', scatter_dimension=1, tiled=True)  143 us
    reduce_scatter x1, waiting for transfers between devices, shards(): lax.psum_scatter(grad_w_in, 'dp', scatter_dimension=0, tiled=True)  142 us
    reduce_scatter x1, waiting for transfers between devices, shards(): lax.psum_scatter(grad_w_out, 'dp', scatter_dimension=1, tiled=True)  126 us
    psum x1, blocking collectives, shards(): lax.psum((grad_bias_qv, grad_bias_out, grad_gain_one, grad_shift_one, gra...  79.8 us
    unnamed x9, waiting for transfers between devices  79 us
    psum x1, waiting for transfers between devices, shards(): lax.psum(attention_part.astype(jnp.bfloat16), 'tensor').astype(jnp.float32)  25.9 us
    psum x1, waiting for transfers between devices, shards(): lax.psum(normed_part.astype(jnp.bfloat16), 'tensor').astype(jnp.float32)  24.5 us
  transfers between devices with their start and end apart: 8, of which 7 were waited for; matrix products, arithmetic and copies ran while one was open for 6% of the time, Pallas kernels for 0%

profile of v1, /device:TPU:0, one launch (start us, length us, event | category | flops | bytes accessed | tf_op | source)
XLA Modules:
  0.0 975.1 jit_solution(13443991043274095177)
XLA Ops:
  7.2 6.5 convolution_bitcast_fusion
  18.2 5.7 squeeze.37
  24.0 5.2 squeeze.38
  36.9 6.5 fusion.77
  44.7 29.7 %while.26 = (s32[]{:T(128)}, bf16[4,512,6,64]{1,3,2,0:T(8,128)(2,1)}, f32[4,6,512]{2,1,0:T(8,128)S(1)}, bf16[4,512,6,64]{1,3,2,0:T(8,128)(2,1)}, pred[4,512,512]...) while((s32[]{:T(128)}, ...), condition=%wide.region_3.4_spmd, body=%wide.region_0.3_spmd.sunk | while | flops 421721088 | bytes 21870684 | solution.py:114
  82.7 25.9 %all-reduce.7.cloned.1.call-done = bf16[2048,768]{1,0:T(8,128)(2,1)} async-done(((bf16[2048,768]{1,0:T(8,128)(2,1)}), bf16[2048,768]{1,0:T(8,128)(2,1)}) %all-reduce.7.cloned.1.call-update) | async-done | bytes 3145744 | tf_op jit(solution)/shard_map/psum | solution.py:117
  108.6 4.1 fusion.73
  115.1 9.6 multiply_convert_fusion.1
  127.4 6.4 convolution_convert_fusion.2
  133.9 18.0 %all-gather.3.cloned.1.call-done = bf16[4096,768]{1,0:T(8,128)(2,1)} async-done(((bf16[2048,768]{1,0:T(8,128)(2,1)}), bf16[4096,768]{1,0:T(8,128)(2,1)}) %all-gather.3.cloned.1.call-update) | async-done | bytes 6291472 | tf_op jit(solution)/shard_map/all_gather | solution.py:127
  151.9 6.4 reduce_sum.185
  158.2 5.6 fusion.96
  173.1 13.6 %convert_reduce_fusion = (f32[1536]{0:T(1024)}, bf16[2048,1536]{1,0:T(8,128)(2,1)S(1)}) fusion(f32[2048,1536]{1,0:T(8,128)} %get-tuple-element.270, f32[1536]{0:T(1024)S(1)} %convert_element_type.150, bf16[1536,768]{1,0:T(8,128)(2,1)S(1)} %copy-done.32, f32[2048,768]{1,0:T(8,128)S(1)} %get-tuple-element.267), kind=kOutput, calls=%fused_computation.71 | convolution fusion | flops 4874304000 | bytes 27537408 | tf_op jit(solution)/shard_map/nd,fd->nf/dot_general | solution.py:142
  189.4 6.4 convolution_convert_fusion.1
  195.9 24.5 %all-reduce.9.cloned.1.call-done = bf16[2048,768]{1,0:T(8,128)(2,1)} async-done(((bf16[2048,768]{1,0:T(8,128)(2,1)}), bf16[2048,768]{1,0:T(8,128)(2,1)}) %all-reduce.9.cloned.1.call-update) | async-done | bytes 3145744 | tf_op jit(solution)/shard_map/psum | solution.py:147
  220.4 7.8 multiply_reduce_fusion.1
  228.2 8.2 fusion.95
  236.4 4.6 convolution_convert_fusion.3
  251.2 64.7 %while.27 = (s32[]{:T(128)}, bf16[4,512,6,64]{1,3,2,0:T(8,128)(2,1)}, bf16[4,512,6,64]{1,3,2,0:T(8,128)(2,1)}, bf16[4,512,6,64]{1,3,2,0:T(8,128)(2,1)}, bf16[4,5...) while((s32[]{:T(128)}, ...), condition=%wide.region_17.18_spmd, body=%wide.region_15.17_spmd.sunk | while | flops 1031205888 | bytes 52520052 | solution.py:161
  315.9 3.9 copy.76
  334.0 9.1 bitcast_convert_fusion
  343.1 8.5 fusion.79
  351.6 6.3 copy.83
  358.0 6.1 fusion.82
  364.4 12.1 %fusion.88 = f32[768,1536]{1,0:T(8,128)} fusion(bf16[2048,1536]{1,0:T(8,128)(2,1)} %copy-done.35, f32[768]{0:T(1024)S(1)} %copy-done.21, f32[768]{0:T(1024)S(1)} %convert_element_type.147, bf16[2048,768]{1,0:T(8,128)(2,1)} %all-reduce.7.cloned.1.call-done, bf16[2048,768]{1,0:T(8,128)(2,1)S(1)} %copy-done.4, f32[2048]{0:T(1024)S(1)} %add_rsqrt_fusion.1, ...), kind=kOutput, calls=%fused_computation.125 | convolution fusion | flops 4845993984 | bytes 17327104 | tf_op jit(solution)/shard_map/nd,nf->df/dot_general | solution.py:145
  376.6 10.6 %fusion.85 = f32[1536,768]{0,1:T(8,128)} fusion(bf16[2048,1536]{1,0:T(8,128)(2,1)} %copy-done.34, f32[2048,768]{1,0:T(8,128)} %copy-done.7), kind=kOutput, calls=%fused_computation.122 | convolution fusion | flops 4833411072 | bytes 17301504 | tf_op jit(solution)/shard_map/nf,nd->fd/dot_general | solution.py:139
  390.7 79.8 %all-reduce.1 = (f32[2,384]{1,0:T(2,128)}, f32[768]{0:T(1024)}, f32[768]{0:T(1024)}, f32[768]{0:T(1024)}, f32[1536]{0:T(1024)}, /*index=5*/f32[768]{0:T(1024)}, f32[768]{0:T(1024)}, f32[768]{0:T(1024)}) all-reduce(f32[2,384]{1,0:T(2,128)S(1)} %pad_maximum_fusion.3, ...), channel_id=1, replica_groups=mesh['dp'=16,'tensor'=2] {'dp'}, use_global_device_ids=true, to_apply=%region_22.23 | all-reduce | flops 6912 | bytes 55296 | tf_op jit(solution)/shard_map/psum | solution.py:200
  470.5 6.2 add_convert_fusion
  476.7 78.9 %all-reduce.13.cloned.1.call-done = f32[3,768,384]{2,0,1:T(4,128)} async-done(((f32[3,768,384]{2,0,1:T(4,128)}), f32[3,768,384]{2,0,1:T(4,128)}) %all-reduce.13.cloned.1.call-update) | async-done | bytes 3538960
  557.4 126.1 %reduce-scatter.4.cloned.1.call-done = f32[384,48]{0,1:T(8,128)} async-done(((f32[384,768]{0,1:T(8,128)}), f32[384,48]{0,1:T(8,128)}) %reduce-scatter.4.cloned.1.call-update) | async-done | bytes 73744 | tf_op jit(solution)/shard_map/reduce_scatter | solution.py:187
  683.4 142.0 %reduce-scatter.6.cloned.1.call-done = f32[48,1536]{1,0:T(8,128)} async-done(((f32[768,1536]{1,0:T(8,128)}), f32[48,1536]{1,0:T(8,128)}) %reduce-scatter.6.cloned.1.call-update) | async-done | bytes 294928 | tf_op jit(solution)/shard_map/reduce_scatter | solution.py:188
  825.5 142.6 %reduce-scatter.8.cloned.1.call-done = f32[1536,48]{0,1:T(8,128)} async-done(((f32[1536,768]{0,1:T(8,128)}), f32[1536,48]{0,1:T(8,128)}) %reduce-scatter.8.cloned.1.call-update) | async-done | bytes 294928 | tf_op jit(solution)/shard_map/reduce_scatter | solution.py:189
  (195 shorter events, 161.5 us)
Async XLA Ops:
  7.2 107.9 %copy-start = (bf16[768,1536]{1,0:T(8,128)(2,1)S(1)}, bf16[768,1536]{1,0:T(8,128)(2,1)}, u32[]{:S(2)}) copy-start(bf16[768,1536]{1,0:T(8,128)(2,1)} %param.27) | copy-start | bytes 7077892
  7.2 101.4 %all-reduce.7.cloned.1.call-start = ((), (), s32[]{:S(2)}) async-start(), calls=%async_computation.3 | async-start | bytes 6291456 | tf_op jit(solution)/shard_map/psum | solution.py:117
  18.2 11.0 %copy-start.23 = (bf16[2,384]{1,0:T(2,128)(2,1)S(1)}, bf16[2,384]{1,0:T(2,128)(2,1)}, u32[]{:S(2)}) copy-start(bf16[2,384]{1,0:T(2,128)(2,1)} %param.22) | copy-start | bytes 4612
  24.0 12.2 %copy-start.17 = (s32[4,512]{1,0:T(4,128)S(1)}, s32[4,512]{1,0:T(4,128)}, u32[]{:S(2)}) copy-start(s32[4,512]{1,0:T(4,128)} %param.20) | copy-start | bytes 24580
  74.4 8.1 copy-start.10
  77.9 4.7 copy-start.26
  77.9 4.7 copy-start.27
  77.9 4.8 copy-start.24
  82.5 69.3 %all-gather.3.cloned.1.call-start = ((), (), s32[]{:S(2)}) async-start(), calls=%async_computation.9 | async-start | bytes 9437184 | tf_op jit(solution)/shard_map/all_gather | solution.py:127
  82.7 75.6 %copy-start.20 = (f32[768]{0:T(1024)}, f32[768]{0:T(1024)S(1)}, u32[]{:S(2)}) copy-start(f32[768]{0:T(1024)S(1)} %convert_element_type.148) | copy-start | bytes 9220
  115.1 12.3 %copy-start.31 = (bf16[1536,768]{1,0:T(8,128)(2,1)S(1)}, bf16[1536,768]{1,0:T(8,128)(2,1)}, u32[]{:S(2)}) copy-start(bf16[1536,768]{1,0:T(8,128)(2,1)} %param.29) | copy-start | bytes 7077892
  127.4 6.5 copy-start.28
  127.4 6.5 copy-start.29
  127.4 6.5 copy-start.30
  133.8 86.6 %all-reduce.9.cloned.1.call-start = ((), (), s32[]{:S(2)}) async-start(), calls=%async_computation.4 | async-start | bytes 6291456 | tf_op jit(solution)/shard_map/psum | solution.py:147
  173.1 13.7 %copy-start.7 = (f32[2048,768]{1,0:T(8,128)}, f32[2048,768]{1,0:T(8,128)S(1)}, u32[]{:S(2)}) copy-start(f32[2048,768]{1,0:T(8,128)S(1)} %get-tuple-element.267) | copy-start | bytes 18874372
  195.8 32.4 %copy-start.3 = (bf16[2048,768]{1,0:T(8,128)(2,1)S(1)}, bf16[2048,768]{1,0:T(8,128)(2,1)}, u32[]{:S(2)}) copy-start(bf16[2048,768]{1,0:T(8,128)(2,1)} %param.19) | copy-start | bytes 9437188
  195.8 274.7 %all-reduce.11.cloned.1.call-start = ((), (), s32[]{:S(2)}) async-start(), calls=%async_computation.5 | async-start | bytes 6291456 | tf_op jit(solution)/shard_map/psum | solution.py:183
  220.4 7.8 copy-start.6
  220.4 7.8 copy-start.12
  228.2 8.2 copy-start.16
  241.8 9.4 copy-start.8
  315.9 8.4 copy-start.13
  334.0 9.2 copy-start.4
  343.1 212.6 %all-reduce.13.cloned.1.call-start = ((), (), s32[]{:S(2)}) async-start(), calls=%async_computation.10 | async-start | bytes 9437184
  357.9 6.5 copy-start.21
  357.9 325.5 %reduce-scatter.4.cloned.1.call-start = ((), (), s32[]{:S(2)}) async-start(), calls=%async_computation.6 | async-start | bytes 1253376 | tf_op jit(solution)/shard_map/reduce_scatter | solution.py:187
  364.1 461.3 %reduce-scatter.6.cloned.1.call-start = ((), (), s32[]{:S(2)}) async-start(), calls=%async_computation.7 | async-start | bytes 5013504 | tf_op jit(solution)/shard_map/reduce_scatter | solution.py:188
  376.5 10.7 %copy-start.33 = (u32[32]{0:T(128)S(1)}, u32[32]{0:T(128)}, u32[]{:S(2)}) copy-start(u32[32]{0:T(128)} %constant.78) | copy-start | bytes 388
  376.5 12.0 %copy-start.9 = (bf16[4,512,6,64]{1,3,2,0:T(8,128)(2,1)S(1)}, bf16[4,512,6,64]{1,3,2,0:T(8,128)(2,1)}, u32[]{:S(2)}) copy-start(bf16[4,512,6,64]{1,3,2,0:T(8,128)(2,1)} %get-tuple-element.108) | copy-start | bytes 4718596
  376.5 591.5 %reduce-scatter.8.cloned.1.call-start = ((), (), s32[]{:S(2)}) async-start(), calls=%async_computation.8 | async-start | bytes 5013504 | tf_op jit(solution)/shard_map/reduce_scatter | solution.py:189
  390.7 577.3 %copy-start.1 = (bf16[768,1536]{1,0:T(8,128)(2,1)S(1)}, bf16[768,1536]{1,0:T(8,128)(2,1)}, u32[]{:S(2)}) copy-start(bf16[768,1536]{1,0:T(8,128)(2,1)} %param.27) | copy-start | bytes 7077892
  (12 other events, 40.7 us)
Sparse Core Ops, SparseCore 0:
  82.6 25.8 all-reduce.6
  133.9 17.9 all-gather.2
  196.0 24.3 all-reduce.8
  343.2 24.3 all-reduce.10
  374.2 181.4 all-reduce.12
  560.8 122.5 reduce-scatter.3
  689.2 136.2 reduce-scatter.5
  832.0 135.9 reduce-scatter.7
